TPU v7x, 256 devices: a whole 4x4x8 slice. The times are simulated.
256 devices in a mesh: chan: 64 (over y, x, z_lo), tm: 4 (over z_hi, core).
Axes of the slice: x: 4, y: 4, z: 8 (z_hi: 2, z_lo: 4; z = z_hi * 4 + z_lo), core: 2. Of those that a mesh axis runs over, the one named last changes fastest.
Arguments:
- samples: int32 [256, 1048576], P('chan', 'tm'), may hold values from -8 to 7
Outputs:
- visibilities: float32 [1024, 2, 256, 256], P(('chan', 'tm'))
All inputs are finite; a program needn't handle non-finite values.
Results may differ from a plain program's by a relative error of at most 0.00055.
Values may be sent and summed in bfloat16 or wider, within the bound.
A program may use at most 128 MiB of HBM per device.

v0:
```python
import jax
import jax.numpy as jnp
from jax import lax
from jax.sharding import PartitionSpec as P

CH = 1024
TAPS = 16


NOISE_POWER = 21.25


def passed_along(block, axis, distance):
    devices = range(lax.axis_size(axis))
    route = [(i - distance, i) for i in devices if i - distance in devices]
    return lax.ppermute(block, axis, route)


def filter_taps(frame_len, tap_count):
    tap_index = jnp.arange(tap_count, dtype=jnp.int32)[:, None]
    sample_index = jnp.arange(frame_len, dtype=jnp.int32)[None, :]
    position = (tap_count - 1 - tap_index) * frame_len + sample_index
    where_at = position.astype(jnp.float32)
    argument = (where_at - jnp.float32(tap_count * frame_len / 2)) / jnp.float32(frame_len)
    window = 0.5 - 0.5 * jnp.cos(2.0 * jnp.pi * where_at / jnp.float32(tap_count * frame_len))
    return (jnp.sinc(argument) * window).astype(jnp.float32)


def fourier_table(frame_len, chan_total):
    sample_index = jnp.arange(frame_len, dtype=jnp.int32)[:, None]
    chan_index = jnp.arange(chan_total, dtype=jnp.int32)[None, :]
    phase_step = sample_index * chan_index % frame_len
    angle = 2.0 * jnp.pi * phase_step.astype(jnp.float32) / jnp.float32(frame_len)
    norm_factor = 1.0 / jnp.sqrt(jnp.float32(frame_len))
    parts = jnp.stack([jnp.cos(angle) * norm_factor, -jnp.sin(angle) * norm_factor], axis=2)
    return parts.reshape(frame_len, 2 * chan_total)


def correlate(chan_block, vis_scale):
    input_count = chan_block.shape[2]
    stacked = chan_block.reshape(chan_block.shape[0], 2 * input_count, chan_block.shape[3])
    gram_all = jnp.einsum("cas,cbs->cab", stacked, stacked, preferred_element_type=jnp.float32)
    real_vis = gram_all[:, :input_count, :input_count] + gram_all[:, input_count:, input_count:]
    imag_vis = gram_all[:, input_count:, :input_count] - gram_all[:, :input_count, input_count:]
    return jnp.stack([real_vis, imag_vis], axis=1) * vis_scale


def body(samples):
    chan_count = lax.axis_size("chan")
    time_count = lax.axis_size("tm")
    frame_len = 2 * CH
    inp_dev = samples.shape[0]
    spec_dev = samples.shape[1] // frame_len
    frames = samples.reshape(inp_dev, spec_dev, frame_len).astype(jnp.float32)
    weights = filter_taps(frame_len, TAPS)
    padded = jnp.pad(frames, ((0, 0), (TAPS - 1, TAPS - 1), (0, 0)))
    frame_total = spec_dev + TAPS - 1
    filtered = jnp.zeros((inp_dev, frame_total, frame_len), jnp.float32)
    for tap_index in range(TAPS):
        lead = TAPS - 1 - tap_index
        filtered = (
            filtered + weights[tap_index][None, None, :] * padded[:, lead : lead + frame_total]
        )
    own_part = filtered[:, :spec_dev]
    tail_part = filtered[:, spec_dev:]
    carried = passed_along(tail_part, "tm", 1)
    own_part = jnp.concatenate([own_part[:, : TAPS - 1] + carried, own_part[:, TAPS - 1 :]], axis=1)
    dft_table = fourier_table(frame_len, CH)
    spectra = jnp.einsum(
        "isn,nc->cis",
        own_part,
        dft_table,
        preferred_element_type=jnp.float32,
        precision=lax.Precision.HIGHEST,
    )
    spectra = spectra.astype(jnp.bfloat16).reshape(
        chan_count, CH // chan_count, 2, inp_dev, spec_dev
    )
    vis_scale = jnp.float32(1.0 / (NOISE_POWER * spec_dev * time_count))
    turned = lax.all_to_all(spectra, "chan", split_axis=0, concat_axis=3, tiled=True)[0]
    return lax.psum_scatter(correlate(turned, vis_scale), "tm", scatter_dimension=0, tiled=True)


def solution(mesh):
    placed = (P("chan", "tm"),)
    return jax.shard_map(
        body,
        mesh=mesh,
        in_specs=placed,
        out_specs=P(("chan", "tm"), None, None, None),
        check_vma=False,
    )
```

profile of v0, /device:TPU:1, one launch (start us, length us, event | category | flops | bytes accessed | tf_op | source)
XLA Modules:
  0.0 546.4 jit_solution(10620438672917269201)
XLA Ops:
  6.5 0.0 all-reduce.4.cloned.1.call-start
  6.5 2.6 convert_element_type.67
  9.1 2.4 copy.18
  11.6 0.7 fusion.50
  12.3 0.1 fusion.60
  12.4 8.7 %fusion.21 = f32[4,143,2048]{2,1,0:T(8,128)S(1)} fusion(f32[4,128,2048]{2,1,0:T(8,128)S(1)} %bitcast.43, f32[2048]{0:T(1024)S(1)} %bitcast.48, f32[2048]{0:T(1024)S(1)} %bitcast.49, f32[2048]{0:T(1024)S(1)} %bitcast.50, f32[2048]{0:T(1024)S(1)} %bitcast.51, f32[2048]{0:T(1024)S(1)} %bitcast.52, f32[2048]{0:T(1024)S(1)} %bitcast.53, f32[2048]{0:T(1024)S(1)} %bitcast.54, ...), kind=kLoop, calls=%fused_computation.44 | loop fusion | flops 36315136 | bytes 9011200 | tf_op jit(solution)/shard_map/add | solution.py:62
  21.1 0.0 copy-start
  21.1 10.4 %collective-permute-start = (f32[4,15,2048]{2,1,0:T(8,128)S(1)}, f32[4,15,2048]{2,1,0:T(8,128)S(1)}, u32[]{:S(2)}, u32[]{:S(2)}) collective-permute-start(f32[4,15,2048]{2,1,0:T(8,128)S(1)} %slice.176), channel_id=1, source_target_pairs={{0,1},{1,2},{2,3},{4,5},{5,6},{6,7},{8,9},{9,10},{10,11},{12,13},{... | collective-permute-start | bytes 1474568 | tf_op jit(solution)/shard_map/ppermute | solution.py:16
  31.5 33.2 %negate_multiply_fusion = (f32[2048,1024,1]{1,0,2:T(8,128)S(1)}, f32[2048,1024,1]{1,0,2:T(8,128)S(1)}) fusion(), kind=kLoop, calls=%fused_computation.24 | loop fusion | flops 35651584 | bytes 16777216 | tf_op jit(solution)/shard_map/mul | solution.py:35
  64.7 0.0 copy-done
  64.7 2.3 slice.177
  67.0 6.0 %pad_maximum_fusion = f32[2048,1024,2]{1,0,2:T(8,128)} fusion(f32[2048,1024,1]{1,0,2:T(8,128)S(1)} %get-tuple-element.23, f32[2048,1024,1]{1,0,2:T(8,128)S(1)} %get-tuple-element.24), kind=kLoop, calls=%fused_computation | loop fusion | flops 4194304 | bytes 33554432 | tf_op jit(solution)/shard_map/stack | solution.py:35
  73.1 25.4 %copy.10 = f32[2048,1024,2]{0,2,1:T(2,128)} copy(f32[2048,1024,2]{1,0,2:T(8,128)} %pad_maximum_fusion) | data formatting | bytes 33554432 | tf_op jit(solution)/shard_map/stack | solution.py:35
  98.4 20.5 %reshape.111 = f32[2048,2048,1]{0,1,2:T(8,128)} reshape(f32[2048,1024,2]{0,2,1:T(2,128)} %copy.10) | data formatting | bytes 33554432 | tf_op jit(solution)/shard_map/reshape | solution.py:36
  118.9 0.0 collective-permute-done
  118.9 1.1 slice_add_fusion.1
  120.0 31.8 %fusion.43 = bf16[2048,4,128]{2,0,1:T(8,128)(2,1)S(1)} fusion(f32[2048,2048,1]{0,1,2:T(8,128)} %reshape.111, f32[4,113,2048]{2,1,0:T(8,128)} %slice.177, f32[4,15,2048]{2,1,0:T(8,128)S(1)} %slice_add_fusion.1), kind=kOutput, calls=%fused_computation.69 | convolution fusion | flops 25771900928 | bytes 23068672 | tf_op jit(solution)/shard_map/isn,nc->cis/dot_general | solution.py:69
  151.9 2.5 copy.11
  154.3 57.4 %all_to_all.15 = bf16[64,16,2,4,128]{4,2,1,3,0:T(2,128)(2,1)S(1)} all-to-all(bf16[64,16,2,4,128]{4,2,1,3,0:T(2,128)(2,1)S(1)} %copy.11), channel_id=1, replica_groups=mesh['chan'=64,'tm'=4] {'chan'}, dimensions={0} | all-to-all | bytes 4194304 | tf_op jit(solution)/shard_map/all_to_all | solution.py:80
  211.7 1.1 copy.12
  212.8 8.1 %fusion.61 = f32[16,512,512]{2,1,0:T(8,128)} fusion(bf16[16,512,128]{2,1,0:T(8,128)(2,1)S(1)} %bitcast.42), kind=kOutput, calls=%fused_computation.99 | convolution fusion | flops 1073741824 | bytes 18874368 | tf_op jit(solution)/shard_map/cas,cbs->cab/dot_general | solution.py:42
  220.9 9.2 %fusion.38 = (f32[16,1,256,256]{3,2,0,1:T(8,128)S(1)}, f32[16,1,256,256]{3,2,0,1:T(8,128)}) fusion(f32[16,512,512]{2,1,0:T(8,128)} %fusion.61), kind=kLoop, calls=%fused_computation.64 | loop fusion | flops 2097152 | bytes 25165824 | tf_op jit(solution)/shard_map/stack | solution.py:45
  230.1 6.5 %maximum_multiply_fusion = f32[16,2,256,256]{3,2,0,1:T(8,128)} fusion(f32[16,1,256,256]{3,2,0,1:T(8,128)} %get-tuple-element.6, f32[16,1,256,256]{3,2,0,1:T(8,128)S(1)} %get-tuple-element.5), kind=kLoop, calls=%fused_computation.23 | loop fusion | flops 4194304 | bytes 16777216 | tf_op jit(solution)/shard_map/mul | solution.py:45
  236.6 0.0 copy-start.1
  236.6 0.0 all-reduce.4.cloned.1.call-update
  236.7 0.6 copy-done.1
  237.3 0.6 dynamic-slice
  238.5 297.8 %all-reduce.4.cloned.1.call-done = f32[16,2,256,256]{3,2,0,1:T(8,128)} async-done(((f32[16,2,256,256]{3,2,0,1:T(8,128)}), f32[16,2,256,256]{3,2,0,1:T(8,128)}) %all-reduce.4.cloned.1.call-update) | async-done | bytes 8388624
  536.3 1.7 constant_dynamic-slice_fusion
  538.1 1.5 copy.13
  (2 shorter events, 0.0 us)
Async XLA Ops:
  6.5 529.8 %all-reduce.4.cloned.1.call-start = ((), (), s32[]{:S(2)}) async-start(), calls=%async_computation.1 | async-start | bytes 16777216
  21.1 43.6 %copy-start = (f32[4,143,2048]{2,1,0:T(8,128)}, f32[4,143,2048]{2,1,0:T(8,128)S(1)}, u32[]{:S(2)}) copy-start(f32[4,143,2048]{2,1,0:T(8,128)S(1)} %fusion.21) | copy-start | bytes 14057476
  21.1 97.8 %collective-permute-start = (f32[4,15,2048]{2,1,0:T(8,128)S(1)}, f32[4,15,2048]{2,1,0:T(8,128)S(1)}, u32[]{:S(2)}, u32[]{:S(2)}) collective-permute-start(f32[4,15,2048]{2,1,0:T(8,128)S(1)} %slice.176), channel_id=1, source_target_pairs={{0,1},{1,2},{2,3},{4,5},{5,6},{6,7},{8,9},{9,10},{10,11},{12,13},{... | collective-permute-start | bytes 1474568 | tf_op jit(solution)/shard_map/ppermute | solution.py:16
  236.6 0.7 copy-start.1
Sparse Core Ops, SparseCore 0:
  236.8 299.5 all-reduce.3
where the time goes:
time: 548 us; the launch traced here: 546 us
  waiting for transfers between devices  298 us (54%)
  other arithmetic  68 us (12%)
  local copies, waits for them, and re-layouts  58.7 us (11%)
  blocking collectives  57.4 us (10%)
  matrix products  39.9 us (7%)
  between operations  14.1 us (3%)
  starting transfers between devices  10.4 us (2%)
    unnamed x2, waiting for transfers between devices  298 us
    all_to_all x1, blocking collectives, body(): lax.all_to_all(spectra, 'chan', split_axis=0, concat_axis=3, tiled=True)[0]  57.4 us
    mul x1, other arithmetic, fourier_table(): -jnp.sin(angle) * norm_factor  33.2 us
    dot_general x1, matrix products, body(): jnp.einsum('isn,nc->cis', own_part, dft_table, preferred_element_type=jnp...  31.8 us
    another operation x1, local copies, waits for them, and re-layouts, fourier_table(): jnp.stack([jnp.cos(angle) * norm_factor, -jnp.sin(angle) * norm_factor],...  25.4 us
    reshape x1, local copies, waits for them, and re-layouts, fourier_table(): return parts.reshape(frame_len, 2 * chan_total)  20.5 us
  transfers between devices with their start and end apart: 2, of which 1 were waited for; matrix products, arithmetic and copies ran while one was open for 16% of the time, Pallas kernels for 0%

commit v1 on v0

v1 whole, which is shorter than its diff:
```python
import functools

import jax
import jax.numpy as jnp
from jax import lax
from jax.experimental import pallas as pl
from jax.experimental.pallas import tpu as pltpu
from jax.sharding import PartitionSpec as P

CH = 1024
TAPS = 16
NOISE_POWER = 21.25
MESH = pl.DeviceIdType.MESH


def filter_taps(frame_len, tap_count):
    tap_index = jnp.arange(tap_count, dtype=jnp.int32)[:, None]
    sample_index = jnp.arange(frame_len, dtype=jnp.int32)[None, :]
    position = (tap_count - 1 - tap_index) * frame_len + sample_index
    where_at = position.astype(jnp.float32)
    argument = (where_at - jnp.float32(tap_count * frame_len / 2)) / jnp.float32(frame_len)
    window = 0.5 - 0.5 * jnp.cos(2.0 * jnp.pi * where_at / jnp.float32(tap_count * frame_len))
    return (jnp.sinc(argument) * window).astype(jnp.float32)


def fourier_table(frame_len, chan_total):
    sample_index = jnp.arange(frame_len, dtype=jnp.int32)[None, :]
    chan_index = jnp.arange(chan_total, dtype=jnp.int32)[:, None]
    phase_step = sample_index * chan_index % frame_len
    angle = 2.0 * jnp.pi * phase_step.astype(jnp.float32) / jnp.float32(frame_len)
    norm_factor = 1.0 / jnp.sqrt(jnp.float32(frame_len))
    parts = jnp.stack([jnp.cos(angle) * norm_factor, -jnp.sin(angle) * norm_factor], axis=1)
    return parts.reshape(2 * chan_total, frame_len)


def exchange_kernel(chans, times, sent_ref, got_ref, send_sem, recv_sem, own_sem):
    total = chans * times
    me = lax.axis_index("chan") * times + lax.axis_index("tm")
    barrier = pltpu.get_barrier_semaphore()

    def greet(step, _):
        peer = lax.rem(me + step, total)
        pl.semaphore_signal(
            barrier, inc=1, device_id=(peer // times, peer % times), device_id_type=MESH
        )
        return 0

    lax.fori_loop(1, total, greet, 0)
    pl.semaphore_wait(barrier, total - 1)
    own = pltpu.make_async_copy(sent_ref.at[me], got_ref.at[me], own_sem)
    own.start()

    def send(step, _):
        peer = lax.rem(me + step, total)
        pltpu.make_async_remote_copy(
            sent_ref.at[peer],
            got_ref.at[me],
            send_sem,
            recv_sem,
            device_id=(peer // times, peer % times),
            device_id_type=MESH,
        ).start()
        return 0

    lax.fori_loop(1, total, send, 0)
    own.wait()
    others = pl.ds(0, total - 1)
    pltpu.make_async_copy(sent_ref.at[others], sent_ref.at[others], send_sem).wait()
    pltpu.make_async_copy(got_ref.at[others], got_ref.at[others], recv_sem).wait()


def exchange(blocks, chans, times):
    return pl.pallas_call(
        functools.partial(exchange_kernel, chans, times),
        out_shape=jax.ShapeDtypeStruct(blocks.shape, blocks.dtype),
        in_specs=[pl.BlockSpec(memory_space=pltpu.VMEM)],
        out_specs=pl.BlockSpec(memory_space=pltpu.VMEM),
        scratch_shapes=[pltpu.SemaphoreType.DMA] * 3,
        compiler_params=pltpu.CompilerParams(
            collective_id=0, has_side_effects=True, vmem_limit_bytes=40 << 20
        ),
    )(blocks)


def body(samples):
    chans = lax.axis_size("chan")
    times = lax.axis_size("tm")
    frame_len = 2 * CH
    inp_dev = samples.shape[0]
    spec_dev = samples.shape[1] // frame_len
    frames = samples.reshape(inp_dev, spec_dev, frame_len).astype(jnp.bfloat16)
    halo = lax.ppermute(
        frames[:, spec_dev - (TAPS - 1) :], "tm", [(i, i + 1) for i in range(times - 1)]
    )
    padded = jnp.concatenate([halo, frames], axis=1)
    weights = filter_taps(frame_len, TAPS)
    filtered = jnp.zeros((inp_dev, spec_dev, frame_len), jnp.float32)
    for tap_index in range(TAPS):
        lead = TAPS - 1 - tap_index
        filtered = filtered + weights[tap_index][None, None, :] * padded[
            :, lead : lead + spec_dev
        ].astype(jnp.float32)
    table = fourier_table(frame_len, CH)
    spectra = jnp.einsum(
        "cn,isn->cis",
        table,
        filtered,
        preferred_element_type=jnp.float32,
        precision=lax.Precision.HIGH,
    )
    own_chans = CH // (chans * times)
    blocks = spectra.astype(jnp.bfloat16).reshape(chans * times, 2 * own_chans, inp_dev, spec_dev)
    got = exchange(blocks, chans, times)
    got = got.reshape(chans, times, own_chans, 2, inp_dev, spec_dev)
    parts = got.transpose(2, 0, 4, 3, 1, 5).reshape(own_chans, chans * inp_dev, 2, times * spec_dev)
    turned = jnp.stack([parts[:, :, 1], -parts[:, :, 0]], axis=2)
    vis_scale = jnp.float32(1.0 / (NOISE_POWER * spec_dev * times))
    real_vis = jnp.einsum("carn,cbrn->cab", parts, parts, preferred_element_type=jnp.float32)
    imag_vis = jnp.einsum("carn,cbrn->cab", turned, parts, preferred_element_type=jnp.float32)
    return jnp.stack([real_vis, imag_vis], axis=1) * vis_scale


def solution(mesh):
    return jax.shard_map(
        body,
        mesh=mesh,
        in_specs=(P("chan", "tm"),),
        out_specs=P(("chan", "tm"), None, None, None),
        check_vma=False,
    )
```

time: 548 us -> 193 us (0.35)
  waiting for transfers between devices: 298 us -> 0.01 us
  Pallas kernels: 0 us -> 58.7 us
  blocking collectives: 57.4 us -> 0 us
  other arithmetic: 68 us -> 37.9 us
  between operations: 14.1 us -> 0.13 us
  matrix products: 39.9 us -> 31.7 us
    unnamed x2 -> x0, waiting for transfers between devices: 298 us -> none
    pallas_call x0 -> x1, Pallas kernels: none -> 58.7 us  [exchange(): pl.pallas_call(functools.partial(exchange_kernel, chans, times), out_shap...]
    all_to_all x1 -> x0, blocking collectives: 57.4 us -> none  [body(): lax.all_to_all(spectra, 'chan', split_axis=0, concat_axis=3, tiled=True)[0]]
    add x2 -> x0, other arithmetic: 9.79 us -> none  [the longest x1 8.69 us: body(): filtered + weights[tap_index][None, None, :] * padded[:, lead:lead + fram...]
    another operation x1 -> x0, other arithmetic: 9.23 us -> none  [correlate(): return jnp.stack([real_vis, imag_vis], axis=1) * vis_scale]
    dot_general x2 -> x3, matrix products: 39.9 us -> 31.7 us  [the longest x1 30.2 us: body(): jnp.einsum('cn,isn->cis', table, filtered, preferred_element_type=jnp.flo...]
    mul x1, other arithmetic: 6.49 us -> 0.25 us  [body(): return jnp.stack([real_vis, imag_vis], axis=1) * vis_scale]
  transfers between devices with their start and end apart: 2 -> 1, of which waited for: 1 -> 0; matrix products, arithmetic and copies ran while one was open for 16% -> 40% of each run, Pallas kernels for 0% -> 0%
where the time goes in v1:
time: 193 us; the launch traced here: 192 us
  Pallas kernels  58.7 us (30%)
  local copies, waits for them, and re-layouts  53.8 us (28%)
  other arithmetic  37.9 us (20%)
  matrix products  31.7 us (16%)
  starting transfers between devices  10.2 us (5%)
    pallas_call x1, Pallas kernels, exchange(): pl.pallas_call(functools.partial(exchange_kernel, chans, times), out_shap...  58.7 us
    mul x1, other arithmetic, fourier_table(): -jnp.sin(angle) * norm_factor  33.1 us
    dot_general x1, matrix products, body(): jnp.einsum('cn,isn->cis', table, filtered, preferred_element_type=jnp.flo...  30.2 us
    another operation x1, local copies, waits for them, and re-layouts, fourier_table(): jnp.stack([jnp.cos(angle) * norm_factor, -jnp.sin(angle) * norm_factor],...  21.3 us
    reshape x1, local copies, waits for them, and re-layouts, fourier_table(): return parts.reshape(2 * chan_total, frame_len)  20.5 us
    ppermute x1, starting transfers between devices, body(): lax.ppermute(frames[:, spec_dev - (TAPS - 1):], 'tm', [(i, i + 1) for i i...  10.2 us
  transfers between devices with their start and end apart: 1, of which 0 were waited for; matrix products, arithmetic and copies ran while one was open for 40% of the time, Pallas kernels for 0%

profile of v1, /device:TPU:1, one launch (start us, length us, event | category | flops | bytes accessed | tf_op | source)
XLA Modules:
  0.0 192.5 jit_solution(13409120864864223907)
XLA Ops:
  0.0 2.6 %convert_element_type.113 = bf16[4,262144]{1,0:T(4,128)(2,1)S(1)} convert(s32[4,262144]{1,0:T(4,128)} %param.1) | non-fusion elementwise | flops 1048576 | bytes 6291456 | tf_op jit(solution)/shard_map/convert_element_type | solution.py:91
  2.6 1.2 copy.16
  3.8 0.1 slice.138
  3.8 10.2 %collective-permute-start = (bf16[4,15,2048]{2,1,0:T(8,128)(2,1)S(1)}, bf16[4,15,2048]{2,1,0:T(8,128)(2,1)S(1)}, u32[]{:S(2)}, u32[]{:S(2)}) collective-permute-start(bf16[4,15,2048]{2,1,0:T(8,128)(2,1)S(1)} %slice.138), channel_id=1, source_target_pairs={{0,1},{1,2},{2,3},{4,5},{5,6},{6,7},{8,9},{9,10},{10,11},{12,13},{... | collective-permute-start | bytes 737288 | tf_op jit(solution)/shard_map/ppermute | solution.py:92
  14.0 33.1 %negate_multiply_fusion = (f32[1024,1,2048]{2,0,1:T(8,128)S(1)}, f32[1024,1,2048]{2,0,1:T(8,128)S(1)}) fusion(), kind=kLoop, calls=%fused_computation.21 | loop fusion | flops 35651584 | bytes 16777216 | tf_op jit(solution)/shard_map/mul | solution.py:32
  47.2 1.2 pad_maximum_fusion
  48.3 21.3 %copy.8 = f32[1024,2,2048]{2,1,0:T(2,128)} copy(f32[1024,2,2048]{2,0,1:T(8,128)S(1)} %pad_maximum_fusion) | data formatting | bytes 33554432 | tf_op jit(solution)/shard_map/stack | solution.py:32
  69.7 20.5 %reshape.116 = f32[2048,2048,1]{1,0,2:T(8,128)} reshape(f32[1024,2,2048]{2,1,0:T(2,128)} %copy.8) | data formatting | bytes 33554432 | tf_op jit(solution)/shard_map/reshape | solution.py:33
  90.2 0.7 fusion.120
  90.9 0.1 fusion.132
  91.0 0.0 collective-permute-done
  91.0 30.2 %fusion.54 = bf16[2048,4,128]{2,0,1:T(8,128)(2,1)} fusion(f32[2048,2048,1]{1,0,2:T(8,128)} %reshape.116, bf16[4,128,2048]{2,1,0:T(8,128)(2,1)S(1)} %bitcast.42, bf16[4,15,2048]{2,1,0:T(8,128)(2,1)S(1)} %collective-permute-done, f32[2048]{0:T(1024)S(1)} %bitcast.44, f32[2048]{0:T(1024)S(1)} %bitcast.45, f32[2048]{0:T(1024)S(1)} %bitcast.46, ...), kind=kOutput, calls=%fused_computation.74 | convolution fusion | flops 12982419456 | bytes 21348352 | tf_op jit(solution)/shard_map/cn,isn->cis/dot_general | solution.py:104
  121.2 3.4 %copy.9 = bf16[2048,4,128]{2,1,0:T(4,128)(2,1)S(1)} copy(bf16[2048,4,128]{2,0,1:T(8,128)(2,1)} %fusion.54) | data formatting | bytes 4194304 | tf_op jit(solution)/shard_map/convert_element_type | solution.py:112
  124.7 58.7 %shard_map.17 = bf16[256,8,4,128]{3,2,1,0:T(4,128)(2,1)S(1)} custom-call(bf16[256,8,4,128]{3,2,1,0:T(4,128)(2,1)S(1)} %bitcast.38), custom_call_target="tpu_custom_call" | custom-call | tf_op jit(solution)/shard_map/pallas_call | solution.py:73
  183.4 2.9 %copy.10 = bf16[4,64,4,2,4,128]{5,4,2,1,3,0:T(4,128)(2,1)} copy(bf16[4,64,4,2,4,128]{5,2,3,0,4,1:T(4,128)(2,1)S(1)} %bitcast.39) | data formatting | bytes 4194304 | tf_op jit(solution)/shard_map/transpose | solution.py:115
  186.3 2.7 %reshape.115 = bf16[4,256,2,512]{3,1,2,0:T(8,128)(2,1)S(1)} reshape(bf16[4,64,4,2,4,128]{5,4,2,1,3,0:T(4,128)(2,1)} %copy.10) | data formatting | bytes 4194304 | tf_op jit(solution)/shard_map/reshape | solution.py:115
  189.1 0.1 fusion.131
  189.2 0.7 convolution_bitcast_fusion
  190.0 0.8 fusion.113
  190.7 0.2 maximum_multiply_fusion
  191.0 1.5 copy.11
  (1 shorter events, 0.0 us)
Async XLA Ops:
  3.8 87.2 %collective-permute-start = (bf16[4,15,2048]{2,1,0:T(8,128)(2,1)S(1)}, bf16[4,15,2048]{2,1,0:T(8,128)(2,1)S(1)}, u32[]{:S(2)}, u32[]{:S(2)}) collective-permute-start(bf16[4,15,2048]{2,1,0:T(8,128)(2,1)S(1)} %slice.138), channel_id=1, source_target_pairs={{0,1},{1,2},{2,3},{4,5},{5,6},{6,7},{8,9},{9,10},{10,11},{12,13},{... | collective-permute-start | bytes 737288 | tf_op jit(solution)/shard_map/ppermute | solution.py:92

commit v2 on v0

v2 whole, which is shorter than its diff:
```python
import functools

import jax
import jax.numpy as jnp
import numpy as np
from jax import lax
from jax.experimental import pallas as pl
from jax.experimental.pallas import tpu as pltpu
from jax.sharding import PartitionSpec as P

CH = 1024
TAPS = 16
NOISE_POWER = 21.25
MESH = pl.DeviceIdType.MESH
LANES = 128
RADIX = 2 * CH // LANES
PAIRS = RADIX // 2
CONTRACT_LANES = (((1,), (1,)), ((), ()))


def filter_table(inputs):
    frame_len = 2 * CH
    position = (TAPS - 1 - np.arange(TAPS))[:, None] * frame_len + np.arange(frame_len)[None, :]
    argument = (position - TAPS * frame_len / 2) / frame_len
    window = 0.5 - 0.5 * np.cos(2.0 * np.pi * position / (TAPS * frame_len))
    weights = (np.sinc(argument) * window).astype(np.float32)
    weights = weights.reshape(TAPS, RADIX, 1, LANES)
    return np.broadcast_to(weights, (TAPS, RADIX, inputs, LANES)).reshape(TAPS, -1, LANES)


def fourier_tables():
    table = np.zeros((PAIRS, 2, 2, CH // RADIX, 2, LANES), np.float64)
    lane = np.arange(LANES)[None, :]
    for q in range(PAIRS):
        for side in range(2):
            residue = (q, RADIX - q if q else PAIRS)[side]
            chan = residue + RADIX * np.arange(CH // RADIX)[:, None]
            angle = 2.0 * np.pi * (chan * lane % (2 * CH)) / (2 * CH)
            cos, sin = np.cos(angle), np.sin(angle)
            if q == 0:
                table[q, side, 0, :, side] = cos
                table[q, side, 1, :, side] = -sin
            else:
                sign = (1, -1)[side]
                table[q, side, 0, :, 0] = cos
                table[q, side, 0, :, 1] = sign * sin
                table[q, side, 1, :, 0] = -sin
                table[q, side, 1, :, 1] = sign * cos
    table = (table / np.sqrt(2.0 * CH)).reshape(PAIRS, 2 * LANES, 2 * LANES).astype(np.float32)
    high = table.astype(jnp.bfloat16)
    low = (table - high.astype(np.float32)).astype(jnp.bfloat16)
    return high, low


def first_stage(x):
    a = [x[n] + x[n + 8] for n in range(8)]
    b = [x[n] - x[n + 8] for n in range(8)]
    out = [None] * 8
    aa = [a[n] + a[n + 4] for n in range(4)]
    ab = [a[n] - a[n + 4] for n in range(4)]
    even, odd = aa[0] + aa[2], aa[1] + aa[3]
    out[0] = (even + odd, even - odd)
    out[4] = (aa[0] - aa[2], aa[3] - aa[1])
    root = float(np.sqrt(0.5))
    plus, minus = (ab[1] + ab[3]) * root, (ab[1] - ab[3]) * root
    out[2] = (ab[0] + minus, -(ab[2] + plus))
    out[6] = (ab[0] - minus, ab[2] - plus)
    d = [b[n] - b[8 - n] for n in range(1, 4)]
    e = [b[n] + b[8 - n] for n in range(1, 4)]
    for k in (1, 3, 5, 7):
        re = b[0]
        im = -b[4] if k % 4 == 1 else b[4]
        for n in range(1, 4):
            re = re + d[n - 1] * float(np.cos(np.pi * k * n / 8))
            im = im - e[n - 1] * float(np.sin(np.pi * k * n / 8))
        out[k] = (re, im)
    return out


def spectra_kernel(
    chans, times, inputs, spec,
    x_hbm, w_ref, high_ref, low_ref, got_ref,
    x_buf, tail_buf, tail_out, halo, halo_wide, wide, y_high, y_low, sent,
    x_sem, tail_sem, halo_send, halo_recv, send_sem, recv_sem, own_sem, all_in,
):
    total = chans * times
    ahead = TAPS - 1
    rows = RADIX * inputs
    groups = rows // 8
    chan, tm = lax.axis_index("chan"), lax.axis_index("tm")
    barrier = pltpu.get_barrier_semaphore()

    tail_copy = pltpu.make_async_copy(x_hbm.at[pl.ds(spec - ahead, ahead)], tail_buf, tail_sem)
    tail_copy.start()

    def piece(g):
        part = pl.ds(pl.multiple_of(g * 8, 8), 8)
        return pltpu.make_async_copy(x_hbm.at[:, part], x_buf.at[:, part], x_sem.at[g])

    for g in range(groups):
        piece(g).start()

    line = chans // times
    row, column = chan // times, chan % times * times + tm

    def row_peer(step):
        at = lax.rem(column + step, line)
        return (row * times + at // times, at % times)

    def column_peer(step):
        return (lax.rem(row + step, line) * times + chan % times, tm)

    def signal(semaphore, peer):
        pl.semaphore_signal(semaphore, inc=1, device_id=peer, device_id_type=MESH)

    for step in range(1, line):
        signal(barrier, row_peer(step))
        signal(barrier, column_peer(step))

    tail_copy.wait()
    for f in range(ahead):
        tail_out[f] = tail_buf[f].astype(jnp.float32).astype(jnp.bfloat16)

    pl.semaphore_wait(barrier, 2 * (line - 1))
    for step in range(1, line):
        signal(all_in, column_peer(step))

    @pl.when(tm < times - 1)
    def _():
        pltpu.make_async_remote_copy(
            tail_out, halo, halo_send, halo_recv,
            device_id=(chan, lax.rem(tm + 1, times)), device_id_type=MESH,
        ).start()

    def filtered(taps, window, base, fresh, r0):
        seq = list(window) + fresh
        for j in range(TAPS):
            acc = taps[0] * seq[ahead + j]
            for p in range(1, TAPS):
                acc = acc + taps[p] * seq[ahead + j - p]
            wide[pl.ds(r0 * spec + base + j, 8, stride=spec), :] = acc
        return tuple(seq[TAPS:])

    def frame(s, r0):
        return x_buf[s, pl.ds(r0, 8), :].astype(jnp.float32)

    def tap_rows(r0):
        return [w_ref[p, pl.ds(r0, 8), :] for p in range(TAPS)]

    def own_frames(g, _):
        r0 = pl.multiple_of(g * 8, 8)
        piece(g).wait()
        taps = tap_rows(r0)
        window = tuple(frame(s, r0) for s in range(1, TAPS))

        def block(n, window):
            base = TAPS + n * TAPS
            fresh = [frame(base + j, r0) for j in range(TAPS)]
            return filtered(taps, window, base, fresh, r0)

        lax.fori_loop(0, spec // TAPS - 1, block, window)
        return 0

    lax.fori_loop(0, groups, own_frames, 0)

    @pl.when(tm > 0)
    def _():
        pltpu.make_async_copy(halo, halo, halo_recv).wait()
        for f in range(ahead):
            halo_wide[f] = halo[f].astype(jnp.float32)

    @pl.when(tm == 0)
    def _():
        for f in range(ahead):
            halo_wide[f] = jnp.zeros((rows, LANES), jnp.float32)

    def first_frames(g, _):
        r0 = pl.multiple_of(g * 8, 8)
        window = [halo_wide[f, pl.ds(r0, 8), :] for f in range(ahead)]
        filtered(tap_rows(r0), window, 0, [frame(j, r0) for j in range(TAPS)], r0)
        return 0

    lax.fori_loop(0, groups, first_frames, 0)

    def butterflies(n, _):
        i, s0 = n // (spec // 16), n % (spec // 16) * 16
        x = [
            wide[pl.ds(pl.multiple_of((row * inputs + i) * spec + s0, 16), 16), :]
            for row in range(RADIX)
        ]
        place = pl.ds(pl.multiple_of(i * spec + s0, 16), 16)
        for q, parts in enumerate(first_stage(x)):
            for part, value in enumerate(parts):
                lanes = pl.ds(part * LANES, LANES)
                high = value.astype(jnp.bfloat16)
                y_high[q, place, lanes] = high
                y_low[q, place, lanes] = (value - high.astype(jnp.float32)).astype(jnp.bfloat16)
        return 0

    lax.fori_loop(0, inputs * spec // 16, butterflies, 0)

    k2_count = CH // RADIX

    def pair(q, _):
        def dot(a, b):
            return lax.dot_general(a, b, CONTRACT_LANES, preferred_element_type=jnp.float32)

        high, low = high_ref[q], low_ref[q]
        out = dot(high, y_high[q]) + dot(high, y_low[q]) + dot(low, y_high[q])
        mirror = jnp.where(q == 0, PAIRS, RADIX - q)
        for side, residue in enumerate((q, mirror)):
            for ri in range(2):
                for i in range(inputs):
                    first = (side * 2 + ri) * k2_count
                    block = out[first : first + k2_count, i * spec : (i + 1) * spec]
                    start = residue * 8 + ri * inputs + i
                    wide[pl.ds(start, k2_count, stride=RADIX * 8), :] = block
        return 0

    lax.fori_loop(0, PAIRS, pair, 0)

    pl.semaphore_wait(all_in, line - 1)

    def pack_and_send(step, _):
        peer = lax.rem(chan + step, chans)
        rows_at = pl.ds(pl.multiple_of(peer * (RADIX * 8), RADIX * 8), RADIX * 8)
        packed = wide[rows_at, :].astype(jnp.bfloat16)
        sent[pl.ds(peer * times, times)] = packed.reshape(times, RADIX // times, 8, LANES)
        for step_t in range(times):
            peer_t = lax.rem(tm + step_t, times)
            source = sent.at[peer * times + peer_t]
            target = got_ref.at[:, tm, chan]

            def remote():
                pltpu.make_async_remote_copy(
                    source, target, send_sem, recv_sem,
                    device_id=(peer, peer_t), device_id_type=MESH,
                ).start()

            if step_t == 0:

                @pl.when(step == 0)
                def _():
                    pltpu.make_async_copy(source, target, own_sem).start()

                pl.when(step > 0)(remote)
            else:
                remote()
        return 0

    lax.fori_loop(0, chans, pack_and_send, 0)

    pltpu.make_async_copy(sent.at[0], sent.at[0], own_sem).wait()
    others = sent.at[pl.ds(0, total - 1)]
    pltpu.make_async_copy(others, others, send_sem).wait()
    pltpu.make_async_copy(others, others, recv_sem).wait()

    @pl.when(tm < times - 1)
    def _():
        pltpu.make_async_copy(tail_out, tail_out, halo_send).wait()


def gram_kernel(scale, got_ref, vis_ref):
    times = got_ref.shape[1]
    lower = lax.broadcasted_iota(jnp.int32, (1, 8, LANES), 1) < 4
    real, imag = [], []
    for t in range(times):
        block = got_ref[0, t].astype(jnp.float32)
        pairs = block.reshape(block.shape[0] // 2, 2, 8, LANES)
        a, b = pairs[:, 0], pairs[:, 1]
        re = jnp.where(lower, a, pltpu.roll(b, 4, 1))
        im = jnp.where(lower, pltpu.roll(a, 4, 1), b)
        real.append(re.reshape(-1, LANES).astype(jnp.bfloat16))
        imag.append(im.reshape(-1, LANES).astype(jnp.bfloat16))
    both = jnp.concatenate(real + imag, axis=1)
    turned = jnp.concatenate(imag + [-part for part in real], axis=1)
    for part, left in enumerate((both, turned)):
        gram = lax.dot_general(left, both, CONTRACT_LANES, preferred_element_type=jnp.float32)
        vis_ref[0, part] = gram * scale


def body(samples):
    chans = lax.axis_size("chan")
    times = lax.axis_size("tm")
    inputs = samples.shape[0]
    spec = samples.shape[1] // (2 * CH)
    rows = RADIX * inputs
    own_chans = CH // (chans * times)
    arranged = samples.reshape(inputs, spec, RADIX, LANES).transpose(1, 2, 0, 3)
    arranged = arranged.reshape(spec, rows, LANES)
    high, low = fourier_tables()
    vmem = pl.BlockSpec(memory_space=pltpu.VMEM)
    got_shape = (own_chans, times, chans, 2 * inputs, LANES)
    got = pl.pallas_call(
        functools.partial(spectra_kernel, chans, times, inputs, spec),
        out_shape=jax.ShapeDtypeStruct(got_shape, jnp.bfloat16),
        in_specs=[pl.BlockSpec(memory_space=pl.ANY), vmem, vmem, vmem],
        out_specs=vmem,
        scratch_shapes=[
            pltpu.VMEM((spec, rows, LANES), jnp.int32),
            pltpu.VMEM((TAPS - 1, rows, LANES), jnp.int32),
            pltpu.VMEM((TAPS - 1, rows, LANES), jnp.bfloat16),
            pltpu.VMEM((TAPS - 1, rows, LANES), jnp.bfloat16),
            pltpu.VMEM((TAPS - 1, rows, LANES), jnp.float32),
            pltpu.VMEM((rows * spec, LANES), jnp.float32),
            pltpu.VMEM((PAIRS, inputs * spec, 2 * LANES), jnp.bfloat16),
            pltpu.VMEM((PAIRS, inputs * spec, 2 * LANES), jnp.bfloat16),
            pltpu.VMEM((chans * times, own_chans, 2 * inputs, LANES), jnp.bfloat16),
            pltpu.SemaphoreType.DMA((rows // 8,)),
        ]
        + [pltpu.SemaphoreType.DMA] * 6
        + [pltpu.SemaphoreType.REGULAR],
        compiler_params=pltpu.CompilerParams(
            collective_id=0, has_side_effects=True, vmem_limit_bytes=48 << 20
        ),
    )(arranged, jnp.asarray(filter_table(inputs)), jnp.asarray(high), jnp.asarray(low))
    scale = float(np.float32(1.0 / (NOISE_POWER * spec * times)))
    return pl.pallas_call(
        functools.partial(gram_kernel, scale),
        grid=(own_chans,),
        out_shape=jax.ShapeDtypeStruct((own_chans, 2, chans * inputs, chans * inputs), jnp.float32),
        in_specs=[pl.BlockSpec((1, *got_shape[1:]), lambda j: (j, 0, 0, 0, 0))],
        out_specs=pl.BlockSpec(
            (1, 2, chans * inputs, chans * inputs), lambda j: (j, 0, 0, 0)
        ),
    )(got)


def solution(mesh):
    return jax.shard_map(
        body,
        mesh=mesh,
        in_specs=(P("chan", "tm"),),
        out_specs=P(("chan", "tm"), None, None, None),
        check_vma=False,
    )
```

time: 548 us -> 81.3 us (0.15)
  waiting for transfers between devices: 298 us -> 0 us
  Pallas kernels: 0 us -> 76.2 us
  other arithmetic: 68 us -> 0 us
  blocking collectives: 57.4 us -> 0 us
  local copies, waits for them, and re-layouts: 58.7 us -> 4.81 us
  matrix products: 39.9 us -> 0 us
  between operations: 14.1 us -> 0.02 us
  starting transfers between devices: 10.4 us -> 0 us
    unnamed x2 -> x0, waiting for transfers between devices: 298 us -> none
    pallas_call x0 -> x2, Pallas kernels: none -> 76.2 us  [the longest x1 71.5 us: body(): pl.pallas_call(functools.partial(spectra_kernel, chans, times, inputs, sp...]
    all_to_all x1 -> x0, blocking collectives: 57.4 us -> none  [body(): lax.all_to_all(spectra, 'chan', split_axis=0, concat_axis=3, tiled=True)[0]]
    mul x4 -> x0, other arithmetic: 40.4 us -> none  [the longest x1 33.2 us: fourier_table(): -jnp.sin(angle) * norm_factor]
    dot_general x2 -> x0, matrix products: 39.9 us -> none  [the longest x1 31.8 us: body(): jnp.einsum('isn,nc->cis', own_part, dft_table, preferred_element_type=jnp...]
    another operation x1 -> x0, local copies, waits for them, and re-layouts: 25.4 us -> none  [fourier_table(): jnp.stack([jnp.cos(angle) * norm_factor, -jnp.sin(angle) * norm_factor],...]
    reshape x2 -> x0, local copies, waits for them, and re-layouts: 23 us -> none  [the longest x1 20.5 us: fourier_table(): return parts.reshape(frame_len, 2 * chan_total)]
    another operation x2 -> x0, other arithmetic: 15.3 us -> none  [the longest x1 9.23 us: correlate(): return jnp.stack([real_vis, imag_vis], axis=1) * vis_scale]
  transfers between devices with their start and end apart: 2 -> 0, of which waited for: 1 -> 0; matrix products, arithmetic and copies ran while one was open for 16% -> 0% of each run, Pallas kernels for 0% -> 0%
where the time goes in v2:
time: 81.3 us; the launch traced here: 81 us
  Pallas kernels  76.2 us (94%)
  local copies, waits for them, and re-layouts  4.81 us (6%)
    pallas_call x1, Pallas kernels, body(): pl.pallas_call(functools.partial(spectra_kernel, chans, times, inputs, sp...  71.5 us
    unnamed x8, local copies, waits for them, and re-layouts  4.81 us
    pallas_call x1, Pallas kernels, body(): pl.pallas_call(functools.partial(gram_kernel, scale), grid=(own_chans,),...  4.68 us

profile of v2, /device:TPU:1, one launch (start us, length us, event | category | flops | bytes accessed | tf_op | source)
XLA Modules:
  0.0 81.0 jit_solution(15890227746772277499)
XLA Ops:
  0.0 0.0 copy-start.1
  0.0 1.2 %copy-done.1 = bf16[8,256,256]{2,1,0:T(8,128)(2,1)S(1)} copy-done((bf16[8,256,256]{2,1,0:T(8,128)(2,1)S(1)}, bf16[8,256,256]{2,1,0:T(8,128)(2,1)}, u32[]{:S(2)}) %copy-start.1) | copy-done | bytes 1048600
  1.2 0.0 copy-start.2
  1.2 1.2 %copy-done.2 = bf16[8,256,256]{2,1,0:T(8,128)(2,1)S(1)} copy-done((bf16[8,256,256]{2,1,0:T(8,128)(2,1)S(1)}, bf16[8,256,256]{2,1,0:T(8,128)(2,1)}, u32[]{:S(2)}) %copy-start.2) | copy-done | bytes 1048600
  2.5 0.0 copy-start.3
  2.5 1.0 %copy-done.3 = f32[16,64,128]{2,1,0:T(8,128)S(1)} copy-done((f32[16,64,128]{2,1,0:T(8,128)S(1)}, f32[16,64,128]{2,1,0:T(8,128)}, u32[]{:S(2)}) %copy-start.3) | copy-done | bytes 524312
  3.5 71.5 %shard_map.46.got_ref = bf16[4,4,64,8,128]{4,3,2,1,0:T(8,128)(2,1)S(1)} custom-call(s32[128,64,128]{2,1,0:T(8,128)} %bitcast.5, f32[16,64,128]{2,1,0:T(8,128)S(1)} %copy-done.3, bf16[8,256,256]{2,1,0:T(8,128)(2,1)S(1)} %copy-done.2, bf16[8,256,256]{2,1,0:T(8,128)(2,1)S(1)} %copy-done.1), custom_call_target="tpu_custom_call" | custom-call | tf_op jit(solution)/shard_map/pallas_call | solution.py:294
  75.0 0.0 copy-start
  75.0 1.3 %copy-done = bf16[4,4,64,8,128]{4,3,2,1,0:T(8,128)(2,1)} copy-done((bf16[4,4,64,8,128]{4,3,2,1,0:T(8,128)(2,1)}, bf16[4,4,64,8,128]{4,3,2,1,0:T(8,128)(2,1)S(1)}, u32[]{:S(2)}) %copy-start) | copy-done | bytes 2097176
  76.3 4.7 %shard_map.47 = f32[4,2,256,256]{3,2,1,0:T(8,128)} custom-call(bf16[4,4,64,8,128]{4,3,2,1,0:T(8,128)(2,1)} %copy-done), custom_call_target="tpu_custom_call" | custom-call | tf_op jit(solution)/shard_map/pallas_call | solution.py:318
Async XLA Ops:
  0.0 1.2 %copy-start.1 = (bf16[8,256,256]{2,1,0:T(8,128)(2,1)S(1)}, bf16[8,256,256]{2,1,0:T(8,128)(2,1)}, u32[]{:S(2)}) copy-start(bf16[8,256,256]{2,1,0:T(8,128)(2,1)} %constant.8.clone.low_ref) | copy-start | bytes 3145732
  1.2 1.2 %copy-start.2 = (bf16[8,256,256]{2,1,0:T(8,128)(2,1)S(1)}, bf16[8,256,256]{2,1,0:T(8,128)(2,1)}, u32[]{:S(2)}) copy-start(bf16[8,256,256]{2,1,0:T(8,128)(2,1)} %constant.7.clone.high_ref) | copy-start | bytes 3145732
  2.5 1.0 %copy-start.3 = (f32[16,64,128]{2,1,0:T(8,128)S(1)}, f32[16,64,128]{2,1,0:T(8,128)}, u32[]{:S(2)}) copy-start(f32[16,64,128]{2,1,0:T(8,128)} %constant.6.clone.w_ref) | copy-start | bytes 1572868
  75.0 1.3 %copy-start = (bf16[4,4,64,8,128]{4,3,2,1,0:T(8,128)(2,1)}, bf16[4,4,64,8,128]{4,3,2,1,0:T(8,128)(2,1)S(1)}, u32[]{:S(2)}) copy-start(bf16[4,4,64,8,128]{4,3,2,1,0:T(8,128)(2,1)S(1)} %shard_map.46.got_ref) | copy-start | bytes 6291460

commit v3 on v2

v3 whole, which is shorter than its diff:
```python
import functools

import jax
import jax.numpy as jnp
import numpy as np
from jax import lax
from jax.experimental import pallas as pl
from jax.experimental.pallas import tpu as pltpu
from jax.sharding import PartitionSpec as P

CH = 1024
TAPS = 16
NOISE_POWER = 21.25
MESH = pl.DeviceIdType.MESH
LANES = 128
RADIX = 2 * CH // LANES
PAIRS = RADIX // 2
CONTRACT_LANES = (((1,), (1,)), ((), ()))


def filter_table(inputs):
    frame_len = 2 * CH
    position = (TAPS - 1 - np.arange(TAPS))[:, None] * frame_len + np.arange(frame_len)[None, :]
    argument = (position - TAPS * frame_len / 2) / frame_len
    window = 0.5 - 0.5 * np.cos(2.0 * np.pi * position / (TAPS * frame_len))
    weights = (np.sinc(argument) * window).astype(np.float32)
    weights = weights.reshape(TAPS, RADIX, 1, LANES)
    return np.broadcast_to(weights, (TAPS, RADIX, inputs, LANES)).reshape(TAPS, -1, LANES)


def fourier_tables():
    table = np.zeros((PAIRS, 2, 2, CH // RADIX, 2, LANES), np.float64)
    lane = np.arange(LANES)[None, :]
    for q in range(PAIRS):
        for side in range(2):
            residue = (q, RADIX - q if q else PAIRS)[side]
            chan = residue + RADIX * np.arange(CH // RADIX)[:, None]
            angle = 2.0 * np.pi * (chan * lane % (2 * CH)) / (2 * CH)
            cos, sin = np.cos(angle), np.sin(angle)
            if q == 0:
                table[q, side, 0, :, side] = cos
                table[q, side, 1, :, side] = -sin
            else:
                sign = (1, -1)[side]
                table[q, side, 0, :, 0] = cos
                table[q, side, 0, :, 1] = sign * sin
                table[q, side, 1, :, 0] = -sin
                table[q, side, 1, :, 1] = sign * cos
    table = (table / np.sqrt(2.0 * CH)).reshape(PAIRS, 2 * LANES, 2 * LANES).astype(np.float32)
    high = table.astype(jnp.bfloat16)
    low = (table - high.astype(np.float32)).astype(jnp.bfloat16)
    return high, low


def first_stage(x):
    a = [x[n] + x[n + 8] for n in range(8)]
    b = [x[n] - x[n + 8] for n in range(8)]
    out = [None] * 8
    aa = [a[n] + a[n + 4] for n in range(4)]
    ab = [a[n] - a[n + 4] for n in range(4)]
    even, odd = aa[0] + aa[2], aa[1] + aa[3]
    out[0] = (even + odd, even - odd)
    out[4] = (aa[0] - aa[2], aa[3] - aa[1])
    root = float(np.sqrt(0.5))
    plus, minus = (ab[1] + ab[3]) * root, (ab[1] - ab[3]) * root
    out[2] = (ab[0] + minus, -(ab[2] + plus))
    out[6] = (ab[0] - minus, ab[2] - plus)
    d = [b[n] - b[8 - n] for n in range(1, 4)]
    e = [b[n] + b[8 - n] for n in range(1, 4)]
    for k in (1, 3, 5, 7):
        re = b[0]
        im = -b[4] if k % 4 == 1 else b[4]
        for n in range(1, 4):
            re = re + d[n - 1] * float(np.cos(np.pi * k * n / 8))
            im = im - e[n - 1] * float(np.sin(np.pi * k * n / 8))
        out[k] = (re, im)
    return out


ORDER = ((1, ()), (0, (0,)), (7, (8,)), (5, ()), (4, (4,)), (3, (12,)), (2, (2, 14)), (6, (6, 10)))
EARLY_GROUPS = 3


def channel_gram(blocks, index, scale):
    lower = lax.broadcasted_iota(jnp.int32, (1, 8, LANES), 1) < 4
    real, imag = [], []
    for block in blocks:
        rows = block[:, index * 8 : index * 8 + 8].astype(jnp.float32)
        pairs = rows.reshape(rows.shape[0] // 2, 2, 8, LANES)
        a, b = pairs[:, 0], pairs[:, 1]
        re = jnp.where(lower, a, pltpu.roll(b, 4, 1))
        im = jnp.where(lower, pltpu.roll(a, 4, 1), b)
        real.append(re.reshape(-1, LANES).astype(jnp.bfloat16))
        imag.append(im.reshape(-1, LANES).astype(jnp.bfloat16))
    both = jnp.concatenate(real + imag, axis=1)
    turned = jnp.concatenate(imag + [-part for part in real], axis=1)
    return [
        lax.dot_general(left, both, CONTRACT_LANES, preferred_element_type=jnp.float32) * scale
        for left in (both, turned)
    ]


def spectra_kernel(
    chans, times, inputs, spec, scale,
    x_hbm, w_hbm, high_hbm, low_hbm, early_ref, late_ref,
    x_buf, w_ref, high_ref, low_ref, tail_buf, tail_out, halo, halo_wide, wide, y_high, y_low,
    sent, first_got,
    x_sem, table_sem, tail_sem, halo_send, halo_recv, send_sem, recv_sem, own_sem, all_in,
):
    total = chans * times
    ahead = TAPS - 1
    rows = RADIX * inputs
    groups = rows // 8
    chan, tm = lax.axis_index("chan"), lax.axis_index("tm")
    barrier = pltpu.get_barrier_semaphore()

    line = chans // times
    row, column = chan // times, chan % times * times + tm

    def row_peer(step):
        at = lax.rem(column + step, line)
        return (row * times + at // times, at % times)

    def column_peer(step):
        return (lax.rem(row + step, line) * times + chan % times, tm)

    def signal(semaphore, peer):
        pl.semaphore_signal(semaphore, inc=1, device_id=peer, device_id_type=MESH)

    def piece(g):
        part = pl.ds(pl.multiple_of(g * 8, 8), 8)
        return pltpu.make_async_copy(x_hbm.at[:, part], x_buf.at[:, part], x_sem.at[g])

    weights_copy = pltpu.make_async_copy(w_hbm, w_ref, table_sem.at[0])
    high_copy = pltpu.make_async_copy(high_hbm, high_ref, table_sem.at[1])
    low_copy = pltpu.make_async_copy(low_hbm, low_ref, table_sem.at[2])
    tail_copy = pltpu.make_async_copy(x_hbm.at[pl.ds(spec - ahead, ahead)], tail_buf, tail_sem)
    weights_copy.start()
    piece(0).start()
    tail_copy.start()
    for g in range(1, groups):
        piece(g).start()
    high_copy.start()
    low_copy.start()

    for step in range(1, line):
        signal(barrier, row_peer(step))
        signal(barrier, column_peer(step))

    def filtered(taps, window, base, fresh, r0):
        seq = list(window) + fresh
        for j in range(TAPS):
            acc = taps[0] * seq[ahead + j]
            for p in range(1, TAPS):
                acc = acc + taps[p] * seq[ahead + j - p]
            wide[pl.ds(r0 * spec + base + j, 8, stride=spec), :] = acc
        return tuple(seq[TAPS:])

    def frame(s, r0):
        return x_buf[s, pl.ds(r0, 8), :].astype(jnp.float32)

    def tap_rows(r0):
        return [w_ref[p, pl.ds(r0, 8), :] for p in range(TAPS)]

    def own_frames(g, _):
        r0 = pl.multiple_of(g * 8, 8)
        piece(g).wait()
        taps = tap_rows(r0)
        window = tuple(frame(s, r0) for s in range(1, TAPS))

        def block(n, window):
            base = TAPS + n * TAPS
            fresh = [frame(base + j, r0) for j in range(TAPS)]
            return filtered(taps, window, base, fresh, r0)

        lax.fori_loop(0, spec // TAPS - 1, block, window)
        return 0

    weights_copy.wait()
    tail_copy.wait()
    for f in range(ahead):
        tail_out[f] = tail_buf[f].astype(jnp.float32).astype(jnp.bfloat16)
    lax.fori_loop(0, EARLY_GROUPS, own_frames, 0)

    pl.semaphore_wait(barrier, 2 * (line - 1))

    @pl.when(tm < times - 1)
    def _():
        pltpu.make_async_remote_copy(
            tail_out, halo, halo_send, halo_recv,
            device_id=(chan, lax.rem(tm + 1, times)), device_id_type=MESH,
        ).start()

    for step in range(1, line):
        signal(all_in, column_peer(step))

    lax.fori_loop(EARLY_GROUPS, groups, own_frames, 0)

    @pl.when(tm > 0)
    def _():
        pltpu.make_async_copy(halo, halo, halo_recv).wait()
        for f in range(ahead):
            halo_wide[f] = halo[f].astype(jnp.float32)

    @pl.when(tm == 0)
    def _():
        for f in range(ahead):
            halo_wide[f] = jnp.zeros((rows, LANES), jnp.float32)

    def first_frames(g, _):
        r0 = pl.multiple_of(g * 8, 8)
        window = [halo_wide[f, pl.ds(r0, 8), :] for f in range(ahead)]
        filtered(tap_rows(r0), window, 0, [frame(j, r0) for j in range(TAPS)], r0)
        return 0

    lax.fori_loop(0, groups, first_frames, 0)

    def butterflies(n, _):
        i, s0 = n // (spec // 16), n % (spec // 16) * 16
        x = [
            wide[pl.ds(pl.multiple_of((row * inputs + i) * spec + s0, 16), 16), :]
            for row in range(RADIX)
        ]
        place = pl.ds(pl.multiple_of(i * spec + s0, 16), 16)
        for q, parts in enumerate(first_stage(x)):
            for part, value in enumerate(parts):
                lanes = pl.ds(part * LANES, LANES)
                high = value.astype(jnp.bfloat16)
                y_high[q, place, lanes] = high
                y_low[q, place, lanes] = (value - high.astype(jnp.float32)).astype(jnp.bfloat16)
        return 0

    lax.fori_loop(0, inputs * spec // 16, butterflies, 0)

    high_copy.wait()
    low_copy.wait()
    pl.semaphore_wait(all_in, line - 1)

    k2_count = CH // RADIX

    def transform(q):
        def dot(a, b):
            return lax.dot_general(a, b, CONTRACT_LANES, preferred_element_type=jnp.float32)

        high, low = high_ref[q], low_ref[q]
        out = dot(high, y_high[q]) + dot(high, y_low[q]) + dot(low, y_high[q])
        for side, residue in enumerate((q, RADIX - q if q else PAIRS)):
            for ri in range(2):
                for i in range(inputs):
                    first = (side * 2 + ri) * k2_count
                    block = out[first : first + k2_count, i * spec : (i + 1) * spec]
                    start = residue * 8 + ri * inputs + i
                    wide[pl.ds(start, k2_count, stride=RADIX * 8), :] = block

    def pack(peer, residue):
        at = pl.ds(pl.multiple_of(peer * (RADIX * 8) + residue * 8, 16), 16)
        place = peer * PAIRS + residue // 2
        sent[place] = wide[at, :].astype(jnp.bfloat16)
        return sent.at[place]

    def deliver(residue):
        peer_t, half = residue // times, residue // 2 % 2
        target = (first_got, late_ref)[half].at[tm, chan]

        def remote(peer, source):
            pltpu.make_async_remote_copy(
                source, target, send_sem, recv_sem.at[half],
                device_id=(peer, peer_t), device_id_type=MESH,
            ).start()

        own = pack(chan, residue)

        @pl.when(tm == peer_t)
        def _():
            pltpu.make_async_copy(own, target, own_sem.at[half]).start()

        @pl.when(tm != peer_t)
        def _():
            remote(chan, own)

        def one(step, _):
            peer = lax.rem(chan + step, chans)
            remote(peer, pack(peer, residue))
            return 0

        lax.fori_loop(1, chans, one, 0)

    for q, complete in ORDER:
        transform(q)
        for residue in complete:
            deliver(residue)

    others = sent.at[pl.ds(0, total - 1)]

    def arrived(half):
        pltpu.make_async_copy(sent.at[0], sent.at[0], own_sem.at[half]).wait()
        pltpu.make_async_copy(others, others, recv_sem.at[half]).wait()

    arrived(0)
    for index in range(2):
        parts = channel_gram([first_got[t] for t in range(times)], index, scale)
        for part, value in enumerate(parts):
            early_ref[index, part] = value
    arrived(1)
    both_halves = sent.at[pl.ds(0, 2 * (total - 1))]
    pltpu.make_async_copy(both_halves, both_halves, send_sem).wait()

    @pl.when(tm < times - 1)
    def _():
        pltpu.make_async_copy(tail_out, tail_out, halo_send).wait()


def late_kernel(scale, early_ref, got_ref, vis_ref, late, early_sem, late_sem):
    early_copy = pltpu.make_async_copy(early_ref, vis_ref.at[pl.ds(0, 2)], early_sem)
    early_copy.start()
    copies = []
    for index in range(2):
        parts = channel_gram([got_ref[t] for t in range(got_ref.shape[0])], index, scale)
        for part, value in enumerate(parts):
            late[index, part] = value
        copies.append(
            pltpu.make_async_copy(late.at[index], vis_ref.at[2 + index], late_sem.at[index])
        )
        copies[-1].start()
    early_copy.wait()
    for copy in copies:
        copy.wait()


def body(samples):
    chans = lax.axis_size("chan")
    times = lax.axis_size("tm")
    inputs = samples.shape[0]
    spec = samples.shape[1] // (2 * CH)
    rows = RADIX * inputs
    all_inputs = chans * inputs
    arranged = samples.reshape(inputs, spec, RADIX, LANES).transpose(1, 2, 0, 3)
    arranged = arranged.reshape(spec, rows, LANES)
    weights = jnp.asarray(filter_table(inputs))
    high, low = (jnp.asarray(table) for table in fourier_tables())
    vmem = pl.BlockSpec(memory_space=pltpu.VMEM)
    hbm = pl.BlockSpec(memory_space=pltpu.HBM)
    scale = float(np.float32(1.0 / (NOISE_POWER * spec * times)))
    got_shape = (times, chans, 4 * inputs, LANES)
    vis_shape = (2, 2, all_inputs, all_inputs)
    early, got = pl.pallas_call(
        functools.partial(spectra_kernel, chans, times, inputs, spec, scale),
        out_shape=(
            jax.ShapeDtypeStruct(vis_shape, jnp.float32),
            jax.ShapeDtypeStruct(got_shape, jnp.bfloat16),
        ),
        in_specs=[hbm] * 4,
        out_specs=(vmem, vmem),
        scratch_shapes=[
            pltpu.VMEM((spec, rows, LANES), jnp.int32),
            pltpu.VMEM(weights.shape, jnp.float32),
            pltpu.VMEM(high.shape, jnp.bfloat16),
            pltpu.VMEM(low.shape, jnp.bfloat16),
            pltpu.VMEM((TAPS - 1, rows, LANES), jnp.int32),
            pltpu.VMEM((TAPS - 1, rows, LANES), jnp.bfloat16),
            pltpu.VMEM((TAPS - 1, rows, LANES), jnp.bfloat16),
            pltpu.VMEM((TAPS - 1, rows, LANES), jnp.float32),
            pltpu.VMEM((rows * spec, LANES), jnp.float32),
            pltpu.VMEM((PAIRS, inputs * spec, 2 * LANES), jnp.bfloat16),
            pltpu.VMEM((PAIRS, inputs * spec, 2 * LANES), jnp.bfloat16),
            pltpu.VMEM((chans * PAIRS, 4 * inputs, LANES), jnp.bfloat16),
            pltpu.VMEM(got_shape, jnp.bfloat16),
            pltpu.SemaphoreType.DMA((rows // 8,)),
            pltpu.SemaphoreType.DMA((3,)),
            pltpu.SemaphoreType.DMA,
            pltpu.SemaphoreType.DMA,
            pltpu.SemaphoreType.DMA,
            pltpu.SemaphoreType.DMA,
            pltpu.SemaphoreType.DMA((2,)),
            pltpu.SemaphoreType.DMA((2,)),
            pltpu.SemaphoreType.REGULAR,
        ],
        compiler_params=pltpu.CompilerParams(
            collective_id=0, has_side_effects=True, vmem_limit_bytes=48 << 20
        ),
    )(arranged, *(pltpu.with_memory_space_constraint(v, pltpu.HBM) for v in (weights, high, low)))
    return pl.pallas_call(
        functools.partial(late_kernel, scale),
        out_shape=jax.ShapeDtypeStruct((4, *vis_shape[1:]), jnp.float32),
        in_specs=[vmem, vmem],
        out_specs=hbm,
        scratch_shapes=[
            pltpu.VMEM(vis_shape, jnp.float32),
            pltpu.SemaphoreType.DMA,
            pltpu.SemaphoreType.DMA((2,)),
        ],
        compiler_params=pltpu.CompilerParams(vmem_limit_bytes=40 << 20),
    )(early, got)


def solution(mesh):
    return jax.shard_map(
        body,
        mesh=mesh,
        in_specs=(P("chan", "tm"),),
        out_specs=P(("chan", "tm"), None, None, None),
        check_vma=False,
    )
```

time: 81.3 us -> 68 us (0.84)
  Pallas kernels: 76.2 us -> 67.9 us
  local copies, waits for them, and re-layouts: 4.81 us -> 0 us
    pallas_call x1, Pallas kernels: 71.5 us -> 66.3 us  [body(): pl.pallas_call(functools.partial(spectra_kernel, chans, times, inputs, sp...]
    unnamed x8 -> x0, local copies, waits for them, and re-layouts: 4.81 us -> none
    pallas_call x1, Pallas kernels: 4.68 us -> 1.59 us  [body(): pl.pallas_call(functools.partial(late_kernel, scale), out_shape=jax.Shape...]
where the time goes in v3:
time: 68 us; the launch traced here: 67.9 us
  Pallas kernels  67.9 us (100%)
    pallas_call x1, Pallas kernels, body(): pl.pallas_call(functools.partial(spectra_kernel, chans, times, inputs, sp...  66.3 us
    pallas_call x1, Pallas kernels, body(): pl.pallas_call(functools.partial(late_kernel, scale), out_shape=jax.Shape...  1.59 us

profile of v3, /device:TPU:1, one launch (start us, length us, event | category | flops | bytes accessed | tf_op | source)
XLA Modules:
  0.0 67.9 jit_solution(12702695963610592482)
XLA Ops:
  0.0 66.3 %shard_map.46 = (f32[2,2,256,256]{3,2,1,0:T(8,128)S(1)}, bf16[4,64,16,128]{3,2,1,0:T(8,128)(2,1)S(1)}) custom-call(s32[128,64,128]{2,1,0:T(8,128)} %bitcast.5, f32[16,64,128]{2,1,0:T(8,128)} %constant.6.clone.w_hbm, bf16[8,256,256]{2,1,0:T(8,128)(2,1)} %constant.7.clone.high_hbm, bf16[8,256,256]{2,1,0:T(8,128)(2,1)} %constant.8.clone.low_hbm), custom_call_target="tpu_custom_call" | custom-call | tf_op jit(solution)/shard_map/pallas_call | solution.py:346
  66.3 1.6 %shard_map.47 = f32[4,2,256,256]{3,2,1,0:T(8,128)} custom-call(f32[2,2,256,256]{3,2,1,0:T(8,128)S(1)} %get-tuple-element.7.early_ref, bf16[4,64,16,128]{3,2,1,0:T(8,128)(2,1)S(1)} %get-tuple-element.8.got_ref), custom_call_target="tpu_custom_call" | custom-call | tf_op jit(solution)/shard_map/pallas_call | solution.py:382

commit v4 on v3

--- a/solution.py
+++ b/solution.py
@@ -78,7 +78,7 @@
 
 
 ORDER = ((1, ()), (0, (0,)), (7, (8,)), (5, ()), (4, (4,)), (3, (12,)), (2, (2, 14)), (6, (6, 10)))
-EARLY_GROUPS = 3
+EARLY_GROUPS = 5
 
 
 def channel_gram(blocks, index, scale):
@@ -145,6 +145,7 @@
 
     for step in range(1, line):
         signal(barrier, row_peer(step))
+    for step in range(1, line):
         signal(barrier, column_peer(step))
 
     def filtered(taps, window, base, fresh, r0):
@@ -177,12 +178,14 @@
         return 0
 
     weights_copy.wait()
+    lax.fori_loop(0, EARLY_GROUPS, own_frames, 0)
     tail_copy.wait()
     for f in range(ahead):
         tail_out[f] = tail_buf[f].astype(jnp.float32).astype(jnp.bfloat16)
-    lax.fori_loop(0, EARLY_GROUPS, own_frames, 0)
 
     pl.semaphore_wait(barrier, 2 * (line - 1))
+    for step in range(1, line):
+        signal(all_in, column_peer(step))
 
     @pl.when(tm < times - 1)
     def _():
@@ -191,32 +194,9 @@
             device_id=(chan, lax.rem(tm + 1, times)), device_id_type=MESH,
         ).start()
 
-    for step in range(1, line):
-        signal(all_in, column_peer(step))
-
     lax.fori_loop(EARLY_GROUPS, groups, own_frames, 0)
 
-    @pl.when(tm > 0)
-    def _():
-        pltpu.make_async_copy(halo, halo, halo_recv).wait()
-        for f in range(ahead):
-            halo_wide[f] = halo[f].astype(jnp.float32)
-
-    @pl.when(tm == 0)
-    def _():
-        for f in range(ahead):
-            halo_wide[f] = jnp.zeros((rows, LANES), jnp.float32)
-
-    def first_frames(g, _):
-        r0 = pl.multiple_of(g * 8, 8)
-        window = [halo_wide[f, pl.ds(r0, 8), :] for f in range(ahead)]
-        filtered(tap_rows(r0), window, 0, [frame(j, r0) for j in range(TAPS)], r0)
-        return 0
-
-    lax.fori_loop(0, groups, first_frames, 0)
-
-    def butterflies(n, _):
-        i, s0 = n // (spec // 16), n % (spec // 16) * 16
+    def butterflies(i, s0):
         x = [
             wide[pl.ds(pl.multiple_of((row * inputs + i) * spec + s0, 16), 16), :]
             for row in range(RADIX)
@@ -230,7 +210,30 @@
                 y_low[q, place, lanes] = (value - high.astype(jnp.float32)).astype(jnp.bfloat16)
         return 0
 
-    lax.fori_loop(0, inputs * spec // 16, butterflies, 0)
+    later = spec // 16 - 1
+    lax.fori_loop(
+        0, inputs * later, lambda n, _: butterflies(n // later, (n % later + 1) * 16), 0
+    )
+
+    @pl.when(tm > 0)
+    def _():
+        pltpu.make_async_copy(halo, halo, halo_recv).wait()
+        for f in range(ahead):
+            halo_wide[f] = halo[f].astype(jnp.float32)
+
+    @pl.when(tm == 0)
+    def _():
+        for f in range(ahead):
+            halo_wide[f] = jnp.zeros((rows, LANES), jnp.float32)
+
+    def first_frames(g, _):
+        r0 = pl.multiple_of(g * 8, 8)
+        window = [halo_wide[f, pl.ds(r0, 8), :] for f in range(ahead)]
+        filtered(tap_rows(r0), window, 0, [frame(j, r0) for j in range(TAPS)], r0)
+        return 0
+
+    lax.fori_loop(0, groups, first_frames, 0)
+    lax.fori_loop(0, inputs, lambda i, _: butterflies(i, 0), 0)
 
     high_copy.wait()
     low_copy.wait()

time: 68 us -> 67.3 us (0.990)
  Pallas kernels: 67.9 us -> 67.2 us
    pallas_call x1, Pallas kernels: 66.3 us -> 65.6 us  [body(): pl.pallas_call(functools.partial(spectra_kernel, chans, times, inputs, sp...]
where the time goes in v4:
time: 67.3 us; the launch traced here: 67.2 us
  Pallas kernels  67.2 us (100%)
    pallas_call x1, Pallas kernels, body(): pl.pallas_call(functools.partial(spectra_kernel, chans, times, inputs, sp...  65.6 us
    pallas_call x1, Pallas kernels, body(): pl.pallas_call(functools.partial(late_kernel, scale), out_shape=jax.Shape...  1.59 us

profile of v4, /device:TPU:1, one launch (start us, length us, event | category | flops | bytes accessed | tf_op | source)
XLA Modules:
  0.0 67.2 jit_solution(18124177601363616880)
XLA Ops:
  0.0 65.6 %shard_map.46 = (f32[2,2,256,256]{3,2,1,0:T(8,128)S(1)}, bf16[4,64,16,128]{3,2,1,0:T(8,128)(2,1)S(1)}) custom-call(s32[128,64,128]{2,1,0:T(8,128)} %bitcast.5, f32[16,64,128]{2,1,0:T(8,128)} %constant.6.clone.w_hbm, bf16[8,256,256]{2,1,0:T(8,128)(2,1)} %constant.7.clone.high_hbm, bf16[8,256,256]{2,1,0:T(8,128)(2,1)} %constant.8.clone.low_hbm), custom_call_target="tpu_custom_call" | custom-call | tf_op jit(solution)/shard_map/pallas_call | solution.py:349
  65.6 1.6 %shard_map.47 = f32[4,2,256,256]{3,2,1,0:T(8,128)} custom-call(f32[2,2,256,256]{3,2,1,0:T(8,128)S(1)} %get-tuple-element.7.early_ref, bf16[4,64,16,128]{3,2,1,0:T(8,128)(2,1)S(1)} %get-tuple-element.8.got_ref), custom_call_target="tpu_custom_call" | custom-call | tf_op jit(solution)/shard_map/pallas_call | solution.py:385

commit v5 on v4

--- a/solution.py
+++ b/solution.py
@@ -237,7 +237,6 @@
 
     high_copy.wait()
     low_copy.wait()
-    pl.semaphore_wait(all_in, line - 1)
 
     k2_count = CH // RADIX
 
@@ -288,8 +287,10 @@
 
         lax.fori_loop(1, chans, one, 0)
 
-    for q, complete in ORDER:
+    for place, (q, complete) in enumerate(ORDER):
         transform(q)
+        if place == 0:
+            pl.semaphore_wait(all_in, line - 1)
         for residue in complete:
             deliver(residue)
 
@@ -363,7 +364,7 @@
             pltpu.VMEM((TAPS - 1, rows, LANES), jnp.bfloat16),
             pltpu.VMEM((TAPS - 1, rows, LANES), jnp.bfloat16),
             pltpu.VMEM((TAPS - 1, rows, LANES), jnp.float32),
-            pltpu.VMEM((rows * spec, LANES), jnp.float32),
+            pltpu.VMEM((rows * spec + spec, LANES), jnp.float32),
             pltpu.VMEM((PAIRS, inputs * spec, 2 * LANES), jnp.bfloat16),
             pltpu.VMEM((PAIRS, inputs * spec, 2 * LANES), jnp.bfloat16),
             pltpu.VMEM((chans * PAIRS, 4 * inputs, LANES), jnp.bfloat16),

time: 67.3 us -> 67.4 us (level)
  no operation moved by 1% of the time
where the time goes in v5:
time: 67.4 us
  Pallas kernels  67.4 us (100%)
    pallas_call x1, Pallas kernels, body(): pl.pallas_call(functools.partial(spectra_kernel, chans, times, inputs, sp...  65.8 us
    pallas_call x1, Pallas kernels, body(): pl.pallas_call(functools.partial(late_kernel, scale), out_shape=jax.Shape...  1.59 us

profile of v5, /device:TPU:1, one launch (start us, length us, event | category | flops | bytes accessed | tf_op | source)
XLA Modules:
  0.0 67.4 jit_solution(11568100252070474625)
XLA Ops:
  0.0 65.8 %shard_map.46 = (f32[2,2,256,256]{3,2,1,0:T(8,128)S(1)}, bf16[4,64,16,128]{3,2,1,0:T(8,128)(2,1)S(1)}) custom-call(s32[128,64,128]{2,1,0:T(8,128)} %bitcast.5, f32[16,64,128]{2,1,0:T(8,128)} %constant.6.clone.w_hbm, bf16[8,256,256]{2,1,0:T(8,128)(2,1)} %constant.7.clone.high_hbm, bf16[8,256,256]{2,1,0:T(8,128)(2,1)} %constant.8.clone.low_hbm), custom_call_target="tpu_custom_call" | custom-call | tf_op jit(solution)/shard_map/pallas_call | solution.py:350
  65.8 1.6 %shard_map.47 = f32[4,2,256,256]{3,2,1,0:T(8,128)} custom-call(f32[2,2,256,256]{3,2,1,0:T(8,128)S(1)} %get-tuple-element.7.early_ref, bf16[4,64,16,128]{3,2,1,0:T(8,128)(2,1)S(1)} %get-tuple-element.8.got_ref), custom_call_target="tpu_custom_call" | custom-call | tf_op jit(solution)/shard_map/pallas_call | solution.py:386
